TPU v7x, 32 devices: a whole 2x2x4 slice. The times are simulated.
32 devices in a mesh: img: 2 (over y), row: 4 (over x, core), col: 4 (over z).
Axes of the slice: x: 2, y: 2, z: 4, core: 2. Of those that a mesh axis runs over, the one named last changes fastest.
Arguments:
- tokens: bfloat16 [4112, 1024], P(('img', 'row'), 'col'), may hold values from -6 to 6
- attn_bias: bfloat16 [16, 257, 257], P('col'), may hold values from -5 to 250
- first_gain: float32 [1024], P('col'), may hold values from 0.5 to 1.5
- first_shift: float32 [1024], P('col'), may hold values from -3 to 3
- qkv_weight: bfloat16 [1024, 3, 1024], P('row', None, 'col'), may hold values from -0.1875 to 0.1875
- qkv_bias: float32 [2, 1024], P(None, 'col'), may hold values from -3 to 3
- proj_weight: bfloat16 [1024, 1024], P('row', 'col'), may hold values from -0.75 to 0.75
- proj_bias: float32 [1024], P('col'), may hold values from -3 to 3
- scale_attn: float32 [1024], P('col'), may hold values from 0.5 to 2
- second_gain: float32 [1024], P('col'), may hold values from 0.5 to 1.5
- second_shift: float32 [1024], P('col'), may hold values from -3 to 3
- fc1_weight: bfloat16 [1024, 4096], P('row', 'col'), may hold values from -0.1875 to 0.1875
- fc1_bias: float32 [4096], P('col'), may hold values from -3 to 3
- fc2_weight: bfloat16 [1024, 4096], P('row', 'col'), may hold values from -0.09375 to 0.09375
- fc2_bias: float32 [1024], P('col'), may hold values from -3 to 3
- scale_mlp: float32 [1024], P('col'), may hold values from 0.5 to 2
- cotangent: float32 [4112, 1024], P(('img', 'row'), 'col'), may hold values from -6 to 6
Outputs:
- out_y: float32 [4112, 1024], P(('img', 'row'), 'col')
- grad_tokens: float32 [4112, 1024], P(('img', 'row'), 'col')
- grad_qkv_weight: float32 [1024, 3, 1024], P('row', None, 'col')
- grad_qkv_bias: float32 [2, 1024], P(None, 'col')
- grad_proj_weight: float32 [1024, 1024], P('row', 'col')
- grad_proj_bias: float32 [1024], P('col')
- grad_scale_attn: float32 [1024], P('col')
- grad_fc1_weight: float32 [1024, 4096], P('row', 'col')
- grad_fc1_bias: float32 [4096], P('col')
- grad_fc2_weight: float32 [1024, 4096], P('row', 'col')
- grad_fc2_bias: float32 [1024], P('col')
- grad_scale_mlp: float32 [1024], P('col')
- grad_first_gain: float32 [1024], P('col')
- grad_first_shift: float32 [1024], P('col')
- grad_second_gain: float32 [1024], P('col')
- grad_second_shift: float32 [1024], P('col')
All inputs are finite; a program needn't handle non-finite values.
Results may differ from a plain program's by a relative error of at most 0.019.
Values may be sent and summed in bfloat16 or wider, within the bound.
No kernel may reach another device: no remote copies, remote signals or barrier semaphores. Data moves between devices by JAX's collectives and lax.ppermute only.
A program may use at most 128 MiB of HBM per device.

v0:
```python
import jax
import jax.numpy as jnp
from jax import lax
from jax.sharding import PartitionSpec as P

HEAD_DIM = 64
D = 1024
SEQ = 257
EPS = 1e-06
SQRT_HALF = 0.7071067811865476
INV_ROOT_TWO_PI = 0.3989422804014327


def gather_cols(values):
    return lax.all_gather(values, "col", axis=1, tiled=True)


def sum_cols(term):
    return lax.psum_scatter(
        term.astype(jnp.bfloat16), "col", scatter_dimension=1, tiled=True
    ).astype(jnp.float32)


def row_totals(sum_one, sum_two):
    return lax.psum((sum_one, sum_two), "col")


def norm_shard(values, gain, shift):
    totals = row_totals(
        jnp.sum(values, axis=1, keepdims=True), jnp.sum(values * values, axis=1, keepdims=True)
    )
    row_mean = totals[0] / D
    row_var = totals[1] / D - row_mean * row_mean
    inv_std = lax.rsqrt(row_var + EPS)
    x_hat = (values - row_mean) * inv_std
    return (x_hat, inv_std, (x_hat * gain + shift).astype(jnp.bfloat16))


def norm_back(grad_in, x_hat, inv_std, gain):
    scaled = grad_in * gain
    totals = row_totals(
        jnp.sum(scaled, axis=1, keepdims=True), jnp.sum(scaled * x_hat, axis=1, keepdims=True)
    )
    return inv_std * (scaled - totals[0] / D - x_hat * (totals[1] / D))


def contract_last(left, right):
    return lax.dot_general(
        left, right, (((1,), (1,)), ((), ())), preferred_element_type=jnp.float32
    )


def contract_first(left, right):
    return lax.dot_general(
        left, right, (((0,), (0,)), ((), ())), preferred_element_type=jnp.float32
    )


def gelu_value(pre_act):
    return 0.5 * pre_act * (1.0 + lax.erf(pre_act * SQRT_HALF))


def gelu_slope(pre_act):
    return (
        0.5 * (1.0 + lax.erf(pre_act * SQRT_HALF))
        + pre_act * jnp.exp(-0.5 * pre_act * pre_act) * INV_ROOT_TWO_PI
    )


def split_heads(heads_in, images, head_count):
    head_grid = heads_in.reshape(images, SEQ, 3, head_count, HEAD_DIM)
    return (head_grid[:, :, 0], head_grid[:, :, 1], head_grid[:, :, 2])


def score_block(query_heads, key_heads, bias_f, score_scale):
    return (
        jnp.einsum("gqhe,gkhe->ghqk", query_heads, key_heads, preferred_element_type=jnp.float32)
        * score_scale
        + bias_f
    )


def attend(heads_in, bias_f, images, head_count, score_scale):
    query_heads, key_heads, value_heads = split_heads(heads_in, images, head_count)
    scores = score_block(query_heads, key_heads, bias_f, score_scale)
    row_max = jnp.max(scores, axis=-1, keepdims=True)
    log_total = row_max + jnp.log(jnp.sum(jnp.exp(scores - row_max), axis=-1, keepdims=True))
    weights_half = jnp.exp(scores - log_total).astype(jnp.bfloat16)
    output = jnp.einsum(
        "ghqk,gkhe->gqhe", weights_half, value_heads, preferred_element_type=jnp.float32
    )
    return (output.reshape(images * SEQ, head_count * HEAD_DIM).astype(jnp.bfloat16), log_total)


def attend_back(heads_in, bias_f, log_total, grad_heads, images, head_count, score_scale):
    query_heads, key_heads, value_heads = split_heads(heads_in, images, head_count)
    scores = score_block(query_heads, key_heads, bias_f, score_scale)
    prob_full = jnp.exp(scores - log_total)
    prob_half = prob_full.astype(jnp.bfloat16)
    grad_out = grad_heads.reshape(images, SEQ, head_count, HEAD_DIM)
    grad_value = jnp.einsum(
        "ghqk,gqhe->gkhe", prob_half, grad_out, preferred_element_type=jnp.float32
    )
    grad_prob = jnp.einsum(
        "gqhe,gkhe->ghqk", grad_out, value_heads, preferred_element_type=jnp.float32
    )
    row_dot = jnp.sum(prob_full * grad_prob, axis=-1, keepdims=True)
    grad_s = (prob_full * (grad_prob - row_dot)).astype(jnp.bfloat16)
    grad_query = (
        jnp.einsum("ghqk,gkhe->gqhe", grad_s, key_heads, preferred_element_type=jnp.float32)
        * score_scale
    )
    grad_key = (
        jnp.einsum("ghqk,gqhe->gkhe", grad_s, query_heads, preferred_element_type=jnp.float32)
        * score_scale
    )
    flat_shape = (images * SEQ, head_count * HEAD_DIM)
    stacked = jnp.stack(
        [
            grad_query.reshape(flat_shape),
            grad_key.reshape(flat_shape),
            grad_value.reshape(flat_shape),
        ],
        axis=1,
    )
    return stacked.astype(jnp.bfloat16)


def body(
    tokens,
    attn_bias,
    first_gain,
    first_shift,
    qkv_weight,
    qkv_bias,
    proj_weight,
    proj_bias,
    scale_attn,
    second_gain,
    second_shift,
    fc1_weight,
    fc1_bias,
    fc2_weight,
    fc2_bias,
    scale_mlp,
    cotangent,
):
    count_rows = tokens.shape[0]
    images = count_rows // SEQ
    head_count = qkv_weight.shape[2] // HEAD_DIM
    score_scale = HEAD_DIM ** (-0.5)
    bias_f = attn_bias.astype(jnp.float32)[None]
    qkv_full, proj_full, hidden_full, output_full = (
        lax.all_gather(qkv_weight, "row", axis=0, tiled=True),
        lax.all_gather(proj_weight, "row", axis=0, tiled=True),
        lax.all_gather(fc1_weight, "row", axis=0, tiled=True),
        lax.all_gather(fc2_weight, "row", axis=0, tiled=True),
    )
    x_val = tokens.astype(jnp.float32)
    hat_first, inv_first, first_local = norm_shard(x_val, first_gain, first_shift)
    first_norm = gather_cols(first_local)
    mixed_all = jnp.einsum("rd,djo->rjo", first_norm, qkv_full, preferred_element_type=jnp.float32)
    heads_in = jnp.stack(
        [mixed_all[:, 0] + qkv_bias[0], mixed_all[:, 1], mixed_all[:, 2] + qkv_bias[1]], axis=1
    ).astype(jnp.bfloat16)
    attn_out, log_total = attend(heads_in, bias_f, images, head_count, score_scale)
    proj_val = sum_cols(contract_last(attn_out, proj_full)) + proj_bias
    x_mid = x_val + scale_attn * proj_val
    hat_second, inv_second, second_local = norm_shard(x_mid, second_gain, second_shift)
    second_norm = gather_cols(second_local)
    pre_act = jnp.dot(second_norm, hidden_full, preferred_element_type=jnp.float32) + fc1_bias
    act_val = gelu_value(pre_act).astype(jnp.bfloat16)
    mlp_val = sum_cols(contract_last(act_val, output_full)) + fc2_bias
    out_y = x_mid + scale_mlp * mlp_val
    qkv_back, proj_back, hidden_back, output_back = (
        lax.all_gather(qkv_weight, "row", axis=0, tiled=True),
        lax.all_gather(proj_weight, "row", axis=0, tiled=True),
        lax.all_gather(fc1_weight, "row", axis=0, tiled=True),
        lax.all_gather(fc2_weight, "row", axis=0, tiled=True),
    )
    grad_mlp = gather_cols((cotangent * scale_mlp).astype(jnp.bfloat16))
    grad_act = jnp.dot(grad_mlp, output_back, preferred_element_type=jnp.float32)
    grad_pre = (grad_act * gelu_slope(pre_act)).astype(jnp.bfloat16)
    grad_two = sum_cols(contract_last(grad_pre, hidden_back))
    grad_mid = cotangent + norm_back(grad_two, hat_second, inv_second, second_gain)
    grad_attn_in = gather_cols((grad_mid * scale_attn).astype(jnp.bfloat16))
    grad_heads = jnp.dot(grad_attn_in, proj_back, preferred_element_type=jnp.float32).astype(
        jnp.bfloat16
    )
    grad_qkv = attend_back(heads_in, bias_f, log_total, grad_heads, images, head_count, score_scale)
    grad_one = sum_cols(
        jnp.einsum("rjo,djo->rd", grad_qkv, qkv_back, preferred_element_type=jnp.float32)
    )
    grad_tokens = grad_mid + norm_back(grad_one, hat_first, inv_first, first_gain)
    grad_terms = (
        jnp.einsum("rd,rjo->djo", first_norm, grad_qkv, preferred_element_type=jnp.float32),
        contract_first(grad_attn_in, attn_out),
        contract_first(second_norm, grad_pre),
        contract_first(grad_mlp, act_val),
    )
    shares = (
        lax.psum_scatter(
            grad_terms[0].astype(jnp.bfloat16), "row", scatter_dimension=0, tiled=True
        ).astype(jnp.float32),
        lax.psum_scatter(
            grad_terms[1].astype(jnp.bfloat16), "row", scatter_dimension=0, tiled=True
        ).astype(jnp.float32),
        lax.psum_scatter(
            grad_terms[2].astype(jnp.bfloat16), "row", scatter_dimension=0, tiled=True
        ).astype(jnp.float32),
        lax.psum_scatter(
            grad_terms[3].astype(jnp.bfloat16), "row", scatter_dimension=0, tiled=True
        ).astype(jnp.float32),
    )
    weight_grads = (
        lax.psum(shares[0].astype(jnp.bfloat16), "img").astype(jnp.float32),
        lax.psum(shares[1].astype(jnp.bfloat16), "img").astype(jnp.float32),
        lax.psum(shares[2].astype(jnp.bfloat16), "img").astype(jnp.float32),
        lax.psum(shares[3].astype(jnp.bfloat16), "img").astype(jnp.float32),
    )
    grad_qkv_f = grad_qkv.astype(jnp.float32)
    small_sums = lax.psum(
        (
            jnp.stack(
                [jnp.sum(grad_qkv_f[:, 0], axis=0), jnp.sum(grad_qkv_f[:, 2], axis=0)], axis=0
            ),
            jnp.sum(grad_mid * scale_attn, axis=0),
            jnp.sum(grad_mid * proj_val, axis=0),
            jnp.sum(grad_pre.astype(jnp.float32), axis=0),
            jnp.sum(cotangent * scale_mlp, axis=0),
            jnp.sum(cotangent * mlp_val, axis=0),
            jnp.sum(grad_one * hat_first, axis=0),
            jnp.sum(grad_one, axis=0),
            jnp.sum(grad_two * hat_second, axis=0),
            jnp.sum(grad_two, axis=0),
        ),
        ("img", "row"),
    )
    return (
        out_y,
        grad_tokens,
        weight_grads[0],
        small_sums[0],
        weight_grads[1],
        small_sums[1],
        small_sums[2],
        weight_grads[2],
        small_sums[3],
        weight_grads[3],
        small_sums[4],
        small_sums[5],
        small_sums[6],
        small_sums[7],
        small_sums[8],
        small_sums[9],
    )


def solution(mesh):
    return jax.shard_map(
        body,
        mesh=mesh,
        in_specs=(
            P(("img", "row"), "col"),
            P("col", None, None),
            P("col"),
            P("col"),
            P("row", None, "col"),
            P(None, "col"),
            P("row", "col"),
            P("col"),
            P("col"),
            P("col"),
            P("col"),
            P("row", "col"),
            P("col"),
            P("row", "col"),
            P("col"),
            P("col"),
            P(("img", "row"), "col"),
        ),
        out_specs=(
            P(("img", "row"), "col"),
            P(("img", "row"), "col"),
            P("row", None, "col"),
            P(None, "col"),
            P("row", "col"),
            P("col"),
            P("col"),
            P("row", "col"),
            P("col"),
            P("row", "col"),
            P("col"),
            P("col"),
            P("col"),
            P("col"),
            P("col"),
            P("col"),
        ),
        check_vma=False,
    )
```

profile of v0, /device:TPU:0, one launch (start us, length us, event | category | flops | bytes accessed | tf_op | source)
XLA Modules:
  0.0 541.6 jit_solution(1392354417559982249)
XLA Ops:
  8.5 13.7 %all-reduce.4 = (f32[514,1]{0,1:T(1,128)S(1)}, f32[514,1]{0,1:T(1,128)S(1)}) all-reduce(f32[514,1]{0,1:T(1,128)S(1)} %broadcast_in_dim.16, f32[514,1]{0,1:T(1,128)S(1)} %broadcast_in_dim.17), channel_id=1, replica_groups=mesh['img'=2,'row'=4,'col'=4] {'col'}, use_global_device_ids=true, to_apply=%region_1.0 | all-reduce | flops 1028 | bytes 8224 | tf_op jit(solution)/shard_map/psum | solution.py:25
  25.0 3.1 copy.51
  28.1 7.6 %all_gather.30 = bf16[1024,256]{1,0:T(8,128)(2,1)} all-gather(bf16[256,256]{1,0:T(8,128)(2,1)S(1)} %copy-done.15), channel_id=1, replica_groups=mesh['img'=2,'row'=4,'col'=4] {'row'}, dimensions={0}, use_global_device_ids=true | all-gather | bytes 655360 | tf_op jit(solution)/shard_map/all_gather | solution.py:155
  35.7 17.0 %all-gather.8.cloned.1.call-done = bf16[514,1024]{1,0:T(8,128)(2,1)} async-done(((bf16[514,256]{1,0:T(8,128)(2,1)}), bf16[514,1024]{1,0:T(8,128)(2,1)}) %all-gather.8.cloned.1.call-update) | async-done | bytes 1052688 | tf_op jit(solution)/shard_map/all_gather | solution.py:15
  52.7 19.5 %all-gather.10.cloned.1.call-done = bf16[1024,3,256]{2,0,1:T(8,128)(2,1)} async-done(((bf16[256,3,256]{2,0,1:T(8,128)(2,1)}), bf16[1024,3,256]{2,0,1:T(8,128)(2,1)}) %all-gather.10.cloned.1.call-update) | async-done | bytes 1572880 | tf_op jit(solution)/shard_map/all_gather | solution.py:154
  91.3 27.3 %reduce-scatter.9.cloned.1.call-done = bf16[514,256]{1,0:T(8,128)(2,1)} async-done(((bf16[514,1024]{1,0:T(8,128)(2,1)}), bf16[514,256]{1,0:T(8,128)(2,1)}) %reduce-scatter.9.cloned.1.call-update) | async-done | bytes 263184 | tf_op jit(solution)/shard_map/reduce_scatter | solution.py:19
  119.8 10.0 %all-reduce.3 = (f32[514,1]{0,1:T(1,128)}, f32[514,1]{0,1:T(1,128)}) all-reduce(f32[514,1]{0,1:T(1,128)S(1)} %broadcast_in_dim.18, f32[514,1]{0,1:T(1,128)S(1)} %broadcast_in_dim.19), channel_id=1, replica_groups=mesh['img'=2,'row'=4,'col'=4] {'col'}, use_global_device_ids=true, to_apply=%region_8.0 | all-reduce | flops 1028 | bytes 8224 | tf_op jit(solution)/shard_map/psum | solution.py:25
  135.3 5.8 %all-gather.14.cloned.1.call-done = bf16[1024,1024]{1,0:T(8,128)(2,1)} async-done(((bf16[256,1024]{1,0:T(8,128)(2,1)}), bf16[1024,1024]{1,0:T(8,128)(2,1)}) %all-gather.14.cloned.1.call-update) | async-done | bytes 2097168 | tf_op jit(solution)/shard_map/all_gather | solution.py:156
  141.1 32.2 %all-gather.12.cloned.1.call-done = bf16[514,1024]{1,0:T(8,128)(2,1)} async-done(((bf16[514,256]{1,0:T(8,128)(2,1)}), bf16[514,1024]{1,0:T(8,128)(2,1)}) %all-gather.12.cloned.1.call-update) | async-done | bytes 1052688 | tf_op jit(solution)/shard_map/all_gather | solution.py:15
  173.3 4.9 multiply_convert_fusion.1
  178.2 25.6 %all-gather.18.cloned.1.call-done = bf16[514,1024]{1,0:T(8,128)(2,1)} async-done(((bf16[514,256]{1,0:T(8,128)(2,1)}), bf16[514,1024]{1,0:T(8,128)(2,1)}) %all-gather.18.cloned.1.call-update) | async-done | bytes 1052688 | tf_op jit(solution)/shard_map/all_gather | solution.py:15
  203.8 22.5 %all-gather.16.cloned.1.call-done = bf16[1024,1024]{1,0:T(8,128)(2,1)} async-done(((bf16[256,1024]{1,0:T(8,128)(2,1)}), bf16[1024,1024]{1,0:T(8,128)(2,1)}) %all-gather.16.cloned.1.call-update) | async-done | bytes 2097168 | tf_op jit(solution)/shard_map/all_gather | solution.py:157
  226.2 5.2 convert_reduce_fusion
  234.8 4.2 convolution_convert_fusion.4
  239.1 23.5 %reduce-scatter.13.cloned.1.call-done = bf16[514,256]{1,0:T(8,128)(2,1)} async-done(((bf16[514,1024]{1,0:T(8,128)(2,1)}), bf16[514,256]{1,0:T(8,128)(2,1)}) %reduce-scatter.13.cloned.1.call-update) | async-done | bytes 263184 | tf_op jit(solution)/shard_map/reduce_scatter | solution.py:19
  264.7 10.0 %all-reduce.2 = (f32[514,1]{0,1:T(1,128)}, f32[514,1]{0,1:T(1,128)}) all-reduce(f32[514,1]{0,1:T(1,128)S(1)} %broadcast_in_dim.21, f32[514,1]{0,1:T(1,128)S(1)} %broadcast_in_dim.20), channel_id=1, replica_groups=mesh['img'=2,'row'=4,'col'=4] {'col'}, use_global_device_ids=true, to_apply=%region_16.0 | all-reduce | flops 1028 | bytes 8224 | tf_op jit(solution)/shard_map/psum | solution.py:25
  275.4 15.9 %reduce-scatter.11.cloned.1.call-done = bf16[514,256]{1,0:T(8,128)(2,1)} async-done(((bf16[514,1024]{1,0:T(8,128)(2,1)}), bf16[514,256]{1,0:T(8,128)(2,1)}) %reduce-scatter.11.cloned.1.call-update) | async-done | bytes 263184 | tf_op jit(solution)/shard_map/reduce_scatter | solution.py:19
  291.3 3.1 multiply_reduce_fusion.2
  296.0 4.7 convolution_convert_fusion
  300.8 4.8 convolution_convert_fusion.1
  306.0 18.9 %all-gather.20.cloned.1.call-done = bf16[514,1024]{1,0:T(8,128)(2,1)} async-done(((bf16[514,256]{1,0:T(8,128)(2,1)}), bf16[514,1024]{1,0:T(8,128)(2,1)}) %all-gather.20.cloned.1.call-update) | async-done | bytes 1052688 | tf_op jit(solution)/shard_map/all_gather | solution.py:15
  331.5 2.8 convolution_convert_fusion.6
  334.2 3.2 fusion.11
  340.3 3.7 multiply_convert_fusion
  352.3 4.0 convolution_convert_fusion.2
  358.4 32.0 %reduce-scatter.21.cloned.1.call-done = bf16[256,1024]{1,0:T(8,128)(2,1)} async-done(((bf16[1024,1024]{1,0:T(8,128)(2,1)}), bf16[256,1024]{1,0:T(8,128)(2,1)}) %reduce-scatter.21.cloned.1.call-update) | async-done | bytes 524304 | tf_op jit(solution)/shard_map/reduce_scatter | solution.py:208
  390.5 24.7 %reduce-scatter.19.cloned.1.call-done = bf16[256,256]{1,0:T(8,128)(2,1)} async-done(((bf16[1024,256]{1,0:T(8,128)(2,1)}), bf16[256,256]{1,0:T(8,128)(2,1)}) %reduce-scatter.19.cloned.1.call-update) | async-done | bytes 131088 | tf_op jit(solution)/shard_map/reduce_scatter | solution.py:205
  415.2 30.4 %reduce-scatter.17.cloned.1.call-done = bf16[256,3,256]{2,0,1:T(8,128)(2,1)} async-done(((bf16[1024,3,256]{2,0,1:T(8,128)(2,1)}), bf16[256,3,256]{2,0,1:T(8,128)(2,1)}) %reduce-scatter.17.cloned.1.call-update) | async-done | bytes 393232 | tf_op jit(solution)/shard_map/reduce_scatter | solution.py:202
  446.0 29.5 %reduce-scatter.15.cloned.1.call-done = bf16[514,256]{1,0:T(8,128)(2,1)} async-done(((bf16[514,1024]{1,0:T(8,128)(2,1)}), bf16[514,256]{1,0:T(8,128)(2,1)}) %reduce-scatter.15.cloned.1.call-update) | async-done | bytes 263184 | tf_op jit(solution)/shard_map/reduce_scatter | solution.py:19
  477.1 24.8 %all-reduce = (f32[2,256]{1,0:T(2,128)}, f32[256]{0:T(256)}, f32[256]{0:T(256)}, f32[1024]{0:T(1024)}, f32[256]{0:T(256)}, /*index=5*/f32[256]{0:T(256)}, f32[25...) all-reduce(f32[2,256]{1,0:T(2,128)S(1)} %pad_maximum_fusion, ...), channel_id=1, replica_groups=mesh['img'=2,'row'=4,'col'=4] {'img','row'}, use_global_device_ids=true, to_apply=%region_27.0 | all-reduce | flops 3584 | bytes 28672 | tf_op jit(solution)/shard_map/psum | solution.py:222
  501.8 9.1 %all-reduce.1 = (f32[514,1]{0,1:T(1,128)S(1)}, f32[514,1]{0,1:T(1,128)S(1)}) all-reduce(f32[514,1]{0,1:T(1,128)S(1)} %broadcast_in_dim.23, f32[514,1]{0,1:T(1,128)S(1)} %broadcast_in_dim.22), channel_id=1, replica_groups=mesh['img'=2,'row'=4,'col'=4] {'col'}, use_global_device_ids=true, to_apply=%region_22.0 | all-reduce | flops 1028 | bytes 8224 | tf_op jit(solution)/shard_map/psum | solution.py:25
  513.1 15.1 %all-reduce.8.cloned.1.call-done = (bf16[256,3,256]{2,0,1:T(8,128)(2,1)}, bf16[256,256]{1,0:T(8,128)(2,1)}, bf16[256,1024]{1,0:T(8,128)(2,1)}, bf16[256,1024]{1,0:T(8,128)(2,1)}) async-done(((bf16[256,3,256]{2,0,1:T(8,128)(2,1)}, bf16[256,256]{1,0:T(8,128)(2,1)}, bf16[256,1024]{1,0:T(8,128)(2,1)}, bf16[256,1024]{1,0:T(8,128)(2,1)}), (bf16[256,3,256]{2,0,1:T(8,128)(2,1)}, bf16[256,256]{1,0:T(8,128)(2,1)}, ...) | async-done | bytes 1572880 | tf_op jit(solution)/shard_map/psum | solution.py:216
  (161 shorter events, 68.3 us)
Async XLA Ops:
  7.2 20.9 %copy-start.15 = (bf16[256,256]{1,0:T(8,128)(2,1)S(1)}, bf16[256,256]{1,0:T(8,128)(2,1)}, u32[]{:S(2)}) copy-start(bf16[256,256]{1,0:T(8,128)(2,1)} %param.23) | copy-start | bytes 393220
  7.2 45.5 %all-gather.8.cloned.1.call-start = ((), (), s32[]{:S(2)}) async-start(), calls=%async_computation.8 | async-start | bytes 1331200 | tf_op jit(solution)/shard_map/all_gather | solution.py:15
  22.2 13.5 %copy-start.27 = (f32[2,256]{1,0:T(2,128)S(1)}, f32[2,256]{1,0:T(2,128)}, u32[]{:S(2)}) copy-start(f32[2,256]{1,0:T(2,128)} %param.22) | copy-start | bytes 6148
  24.2 48.1 %all-gather.10.cloned.1.call-start = ((), (), s32[]{:S(2)}) async-start(), calls=%async_computation.9 | async-start | bytes 1966080 | tf_op jit(solution)/shard_map/all_gather | solution.py:154
  24.9 93.6 %reduce-scatter.9.cloned.1.call-start = ((), (), s32[]{:S(2)}) async-start(), calls=%async_computation.10 | async-start | bytes 1331200 | tf_op jit(solution)/shard_map/reduce_scatter | solution.py:19
  85.9 32.7 %copy-start.2 = (bf16[514,256]{1,0:T(8,128)(2,1)S(1)}, bf16[514,256]{1,0:T(8,128)(2,1)}, u32[]{:S(2)}) copy-start(bf16[514,256]{1,0:T(8,128)(2,1)} %param.17) | copy-start | bytes 789508
  85.9 32.7 %copy-start.16 = (f32[256]{0:T(256)S(1)}, f32[256]{0:T(256)}, u32[]{:S(2)}) copy-start(f32[256]{0:T(256)} %param.25) | copy-start | bytes 3076
  85.9 32.7 %copy-start.17 = (f32[256]{0:T(256)S(1)}, f32[256]{0:T(256)}, u32[]{:S(2)}) copy-start(f32[256]{0:T(256)} %param.24) | copy-start | bytes 3076
  87.9 42.6 %copy-start.18 = (f32[256]{0:T(256)S(1)}, f32[256]{0:T(256)}, u32[]{:S(2)}) copy-start(f32[256]{0:T(256)} %param.26) | copy-start | bytes 3076
  90.7 50.4 %all-gather.14.cloned.1.call-start = ((), (), s32[]{:S(2)}) async-start(), calls=%async_computation.12 | async-start | bytes 2621440 | tf_op jit(solution)/shard_map/all_gather | solution.py:156
  91.2 82.0 %all-gather.12.cloned.1.call-start = ((), (), s32[]{:S(2)}) async-start(), calls=%async_computation.11 | async-start | bytes 1331200 | tf_op jit(solution)/shard_map/all_gather | solution.py:15
  132.4 71.3 %all-gather.18.cloned.1.call-start = ((), (), s32[]{:S(2)}) async-start(), calls=%async_computation.15 | async-start | bytes 1331200 | tf_op jit(solution)/shard_map/all_gather | solution.py:15
  134.3 91.9 %all-gather.16.cloned.1.call-start = ((), (), s32[]{:S(2)}) async-start(), calls=%async_computation.13 | async-start | bytes 2621440 | tf_op jit(solution)/shard_map/all_gather | solution.py:157
  135.1 91.1 %copy-start.30 = (f32[1024]{0:T(1024)S(1)}, f32[1024]{0:T(1024)}, u32[]{:S(2)}) copy-start(f32[1024]{0:T(1024)} %param.29) | copy-start | bytes 12292
  135.1 127.5 %reduce-scatter.13.cloned.1.call-start = ((), (), s32[]{:S(2)}) async-start(), calls=%async_computation.16 | async-start | bytes 1331200 | tf_op jit(solution)/shard_map/reduce_scatter | solution.py:19
  234.7 56.5 %reduce-scatter.11.cloned.1.call-start = ((), (), s32[]{:S(2)}) async-start(), calls=%async_computation.14 | async-start | bytes 1331200 | tf_op jit(solution)/shard_map/reduce_scatter | solution.py:19
  239.1 85.8 %all-gather.20.cloned.1.call-start = ((), (), s32[]{:S(2)}) async-start(), calls=%async_computation.17 | async-start | bytes 1331200 | tf_op jit(solution)/shard_map/all_gather | solution.py:15
  296.0 62.5 %reduce-scatter.23.cloned.1.call-start = ((), (), s32[]{:S(2)}) async-start(), calls=%async_computation.22 | async-start | bytes 2621440 | tf_op jit(solution)/shard_map/reduce_scatter | solution.py:211
  300.8 89.7 %reduce-scatter.21.cloned.1.call-start = ((), (), s32[]{:S(2)}) async-start(), calls=%async_computation.21 | async-start | bytes 2621440 | tf_op jit(solution)/shard_map/reduce_scatter | solution.py:208
  305.7 109.5 %reduce-scatter.19.cloned.1.call-start = ((), (), s32[]{:S(2)}) async-start(), calls=%async_computation.20 | async-start | bytes 655360 | tf_op jit(solution)/shard_map/reduce_scatter | solution.py:205
  340.3 105.4 %reduce-scatter.17.cloned.1.call-start = ((), (), s32[]{:S(2)}) async-start(), calls=%async_computation.19 | async-start | bytes 1966080 | tf_op jit(solution)/shard_map/reduce_scatter | solution.py:202
  356.3 119.3 %reduce-scatter.15.cloned.1.call-start = ((), (), s32[]{:S(2)}) async-start(), calls=%async_computation.18 | async-start | bytes 1331200 | tf_op jit(solution)/shard_map/reduce_scatter | solution.py:19
  358.4 169.8 %all-reduce.8.cloned.1.call-start = ((), (), s32[]{:S(2)}) async-start(), calls=%async_computation.23 | async-start | bytes 3145728 | tf_op jit(solution)/shard_map/psum | solution.py:216
  445.7 29.9 %copy-start.19 = (f32[256]{0:T(256)S(1)}, f32[256]{0:T(256)}, u32[]{:S(2)}) copy-start(f32[256]{0:T(256)} %param.19) | copy-start | bytes 3076
  445.7 31.3 %copy-start.20 = (f32[256]{0:T(256)S(1)}, f32[256]{0:T(256)}, u32[]{:S(2)}) copy-start(f32[256]{0:T(256)} %get-tuple-element.26) | copy-start | bytes 3076
  445.7 31.3 %copy-start.21 = (f32[256]{0:T(256)S(1)}, f32[256]{0:T(256)}, u32[]{:S(2)}) copy-start(f32[256]{0:T(256)} %get-tuple-element.27) | copy-start | bytes 3076
  445.7 31.3 %copy-start.22 = (f32[256]{0:T(256)S(1)}, f32[256]{0:T(256)}, u32[]{:S(2)}) copy-start(f32[256]{0:T(256)} %get-tuple-element.64) | copy-start | bytes 3076
  445.7 31.3 %copy-start.23 = (f32[256]{0:T(256)S(1)}, f32[256]{0:T(256)}, u32[]{:S(2)}) copy-start(f32[256]{0:T(256)} %get-tuple-element.65) | copy-start | bytes 3076
  445.7 31.3 %copy-start.24 = (f32[256]{0:T(256)S(1)}, f32[256]{0:T(256)}, u32[]{:S(2)}) copy-start(f32[256]{0:T(256)} %get-tuple-element.18) | copy-start | bytes 3076
  445.7 31.3 %copy-start.25 = (f32[256]{0:T(256)S(1)}, f32[256]{0:T(256)}, u32[]{:S(2)}) copy-start(f32[256]{0:T(256)} %get-tuple-element.30) | copy-start | bytes 3076
  445.8 31.3 %copy-start.26 = (f32[1024]{0:T(1024)S(1)}, f32[1024]{0:T(1024)}, u32[]{:S(2)}) copy-start(f32[1024]{0:T(1024)} %get-tuple-element.74) | copy-start | bytes 12292
  445.8 65.2 %copy-start.7 = (f32[514,256]{1,0:T(8,128)S(1)}, f32[514,256]{1,0:T(8,128)}, u32[]{:S(2)}) copy-start(f32[514,256]{1,0:T(8,128)} %copy-done.6) | copy-start | bytes 1579012
  (16 other events, 46.1 us)
Sparse Core Ops, SparseCore 0:
  24.3 28.3 all-gather.7
  54.3 17.9 all-gather.9
  90.8 27.7 reduce-scatter.8
  120.0 21.0 all-gather.13
  143.0 30.1 all-gather.11
  175.2 28.4 all-gather.17
  205.3 20.8 all-gather.15
  234.9 27.7 reduce-scatter.12
  264.9 26.3 reduce-scatter.10
  296.1 28.7 all-gather.19
  327.4 29.4 reduce-scatter.22
  359.2 31.1 reduce-scatter.20
  393.5 21.6 reduce-scatter.18
  417.6 28.0 reduce-scatter.16
  447.8 27.7 reduce-scatter.14
  477.9 50.2 all-reduce.7
where the time goes:
time: 543 us; the launch traced here: 542 us
  waiting for transfers between devices  342 us (63%)
  blocking collectives  75.2 us (14%)
  matrix products  54 us (10%)
  other arithmetic  31.2 us (6%)
  local copies, waits for them, and re-layouts  23.8 us (4%)
  between operations  14.5 us (3%)
    reduce_scatter x4, waiting for transfers between devices, sum_cols(): lax.psum_scatter(term.astype(jnp.bfloat16), 'col', scatter_dimension=1, t...  96.2 us
    all_gather x4, waiting for transfers between devices, gather_cols(): return lax.all_gather(values, 'col', axis=1, tiled=True)  93.6 us
    psum x4, blocking collectives, row_totals(): return lax.psum((sum_one, sum_two), 'col')  42.8 us
    reduce_scatter x1, waiting for transfers between devices, body(): lax.psum_scatter(grad_terms[2].astype(jnp.bfloat16), 'row', scatter_dimen...  32 us
    reduce_scatter x1, waiting for transfers between devices, body(): lax.psum_scatter(grad_terms[0].astype(jnp.bfloat16), 'row', scatter_dimen...  30.4 us
    psum x1, blocking collectives, body(): lax.psum((jnp.stack([jnp.sum(grad_qkv_f[:, 0], axis=0), jnp.sum(grad_qkv_...  24.8 us
    reduce_scatter x1, waiting for transfers between devices, body(): lax.psum_scatter(grad_terms[1].astype(jnp.bfloat16), 'row', scatter_dimen...  24.7 us
    all_gather x1, waiting for transfers between devices, body(): lax.all_gather(fc2_weight, 'row', axis=0, tiled=True)  22.5 us
  transfers between devices with their start and end apart: 16, of which 15 were waited for; matrix products, arithmetic and copies ran while one was open for 12% of the time, Pallas kernels for 0%

commit v1 on v0

--- a/solution.py
+++ b/solution.py
@@ -12,7 +12,24 @@
 
 
 def gather_cols(values):
-    return lax.all_gather(values, "col", axis=1, tiled=True)
+
+    def run_yards(field):
+        f_now = lax.axis_size("col")
+        local_part = lax.axis_index("col")
+        outcome_arr, current_block = (f_now, local_part)
+        shaped, x_next = (field, 1)
+        while x_next < outcome_arr:
+            block_out = range(outcome_arr)
+            next_value = map(lambda idx: (idx, idx ^ x_next), block_out)
+            latest = list(next_value)
+            piece_out = lax.ppermute(shaped, axis_name="col", perm=latest)
+            u_next = jnp.concatenate([shaped, piece_out], axis=1)
+            long_array = jnp.concatenate([piece_out, shaped], axis=1)
+            shaped = jnp.where(current_block & x_next == 0, u_next, long_array)
+            x_next = 2 * x_next
+        return shaped
+
+    return run_yards(values)
 
 
 def sum_cols(term):

time: 543 us -> 484 us (0.89)
  waiting for transfers between devices: 342 us -> 276 us
  starting transfers between devices: 1.05 us -> 8.96 us
    all_gather x4 -> x0, waiting for transfers between devices: 93.6 us -> none  [gather_cols(): return lax.all_gather(values, 'col', axis=1, tiled=True)]
    ppermute x0 -> x8, waiting for transfers between devices: none -> 89.7 us  [run_yards(): piece_out = lax.ppermute(shaped, axis_name='col', perm=latest)]
    reduce_scatter x1, waiting for transfers between devices: 24.7 us -> 0.02 us  [body(): lax.psum_scatter(grad_terms[1].astype(jnp.bfloat16), 'row', scatter_dimen...]
    all_gather x1, waiting for transfers between devices: 22.5 us -> 0.01 us  [body(): lax.all_gather(fc2_weight, 'row', axis=0, tiled=True)]
    all_gather x1, waiting for transfers between devices: 19.5 us -> 0.01 us  [body(): lax.all_gather(qkv_weight, 'row', axis=0, tiled=True)]
    reduce_scatter x1, waiting for transfers between devices: 0.02 us -> 12.3 us  [body(): lax.psum_scatter(grad_terms[3].astype(jnp.bfloat16), 'row', scatter_dimen...]
    ppermute x0 -> x8, starting transfers between devices: none -> 8.25 us  [run_yards(): piece_out = lax.ppermute(shaped, axis_name='col', perm=latest)]
    all_gather x1, waiting for transfers between devices: 5.76 us -> 0.01 us  [body(): lax.all_gather(fc1_weight, 'row', axis=0, tiled=True)]
  transfers between devices with their start and end apart: 16 -> 20, of which waited for: 15 -> 16; matrix products, arithmetic and copies ran while one was open for 12% -> 14% of each run, Pallas kernels for 0% -> 0%
where the time goes in v1:
time: 484 us; the launch traced here: 483 us
  waiting for transfers between devices  276 us (57%)
  blocking collectives  75.6 us (16%)
  matrix products  55 us (11%)
  other arithmetic  27.4 us (6%)
  local copies, waits for them, and re-layouts  25.9 us (5%)
  between operations  14.9 us (3%)
  starting transfers between devices  8.96 us (2%)
    reduce_scatter x4, waiting for transfers between devices, sum_cols(): lax.psum_scatter(term.astype(jnp.bfloat16), 'col', scatter_dimension=1, t...  92.3 us
    ppermute x8, waiting for transfers between devices, run_yards(): piece_out = lax.ppermute(shaped, axis_name='col', perm=latest)  89.7 us
    psum x4, blocking collectives, row_totals(): return lax.psum((sum_one, sum_two), 'col')  43.2 us
    reduce_scatter x1, waiting for transfers between devices, body(): lax.psum_scatter(grad_terms[2].astype(jnp.bfloat16), 'row', scatter_dimen...  33.7 us
    reduce_scatter x1, waiting for transfers between devices, body(): lax.psum_scatter(grad_terms[0].astype(jnp.bfloat16), 'row', scatter_dimen...  30.5 us
    psum x1, blocking collectives, body(): lax.psum((jnp.stack([jnp.sum(grad_qkv_f[:, 0], axis=0), jnp.sum(grad_qkv_...  24.8 us
    psum x1, waiting for transfers between devices, body(): lax.psum(shares[0].astype(jnp.bfloat16), 'img').astype(jnp.float32)  15 us
    reduce_scatter x1, waiting for transfers between devices, body(): lax.psum_scatter(grad_terms[3].astype(jnp.bfloat16), 'row', scatter_dimen...  12.3 us
  transfers between devices with their start and end apart: 20, of which 16 were waited for; matrix products, arithmetic and copies ran while one was open for 14% of the time, Pallas kernels for 0%

profile of v1, /device:TPU:0, one launch (start us, length us, event | category | flops | bytes accessed | tf_op | source)
XLA Modules:
  0.0 483.4 jit_solution(8107249804830968896)
XLA Ops:
  9.2 13.8 %all-reduce.4 = (f32[514,1]{0,1:T(1,128)S(1)}, f32[514,1]{0,1:T(1,128)S(1)}) all-reduce(f32[514,1]{0,1:T(1,128)S(1)} %broadcast_in_dim.16, f32[514,1]{0,1:T(1,128)S(1)} %broadcast_in_dim.17), channel_id=1, replica_groups=mesh['img'=2,'row'=4,'col'=4] {'col'}, use_global_device_ids=true, to_apply=%region_1.0 | all-reduce | flops 1028 | bytes 8224 | tf_op jit(solution)/shard_map/psum | solution.py:42
  24.4 6.4 %collective-permute-done = bf16[514,256]{1,0:T(8,128)(2,1)S(1)} collective-permute-done((bf16[514,256]{1,0:T(8,128)(2,1)S(1)}, bf16[514,256]{1,0:T(8,128)(2,1)S(1)}, u32[]{:S(2)}, u32[]{:S(2)}) %collective-permute-start) | collective-permute-done | bytes 263200 | tf_op jit(solution)/shard_map/ppermute | solution.py:25
  33.2 7.6 %all_gather.17 = bf16[1024,256]{1,0:T(8,128)(2,1)} all-gather(bf16[256,256]{1,0:T(8,128)(2,1)S(1)} %copy-done.19), channel_id=1, replica_groups=mesh['img'=2,'row'=4,'col'=4] {'row'}, dimensions={0}, use_global_device_ids=true | all-gather | bytes 655360 | tf_op jit(solution)/shard_map/all_gather | solution.py:172
  40.9 13.1 %collective-permute-done.1 = bf16[514,512]{1,0:T(8,128)(2,1)S(1)} collective-permute-done((bf16[514,512]{1,0:T(8,128)(2,1)S(1)}, bf16[514,512]{1,0:T(8,128)(2,1)S(1)}, u32[]{:S(2)}, u32[]{:S(2)}) %collective-permute-start.1) | collective-permute-done | bytes 526368 | tf_op jit(solution)/shard_map/ppermute | solution.py:25
  73.8 24.7 %reduce-scatter.9.cloned.1.call-done = bf16[514,256]{1,0:T(8,128)(2,1)} async-done(((bf16[514,1024]{1,0:T(8,128)(2,1)}), bf16[514,256]{1,0:T(8,128)(2,1)}) %reduce-scatter.9.cloned.1.call-update) | async-done | bytes 263184 | tf_op jit(solution)/shard_map/reduce_scatter | solution.py:36
  99.8 10.2 %all-reduce.3 = (f32[514,1]{0,1:T(1,128)}, f32[514,1]{0,1:T(1,128)}) all-reduce(f32[514,1]{0,1:T(1,128)S(1)} %broadcast_in_dim.18, f32[514,1]{0,1:T(1,128)S(1)} %broadcast_in_dim.19), channel_id=1, replica_groups=mesh['img'=2,'row'=4,'col'=4] {'col'}, use_global_device_ids=true, to_apply=%region_8.9 | all-reduce | flops 1028 | bytes 8224 | tf_op jit(solution)/shard_map/psum | solution.py:42
  113.0 5.4 %collective-permute-done.2 = bf16[514,256]{1,0:T(8,128)(2,1)S(1)} collective-permute-done((bf16[514,256]{1,0:T(8,128)(2,1)S(1)}, bf16[514,256]{1,0:T(8,128)(2,1)S(1)}, u32[]{:S(2)}, u32[]{:S(2)}) %collective-permute-start.2) | collective-permute-done | bytes 263200 | tf_op jit(solution)/shard_map/ppermute | solution.py:25
  121.8 12.3 %collective-permute-done.4 = bf16[514,256]{1,0:T(8,128)(2,1)S(1)} collective-permute-done((bf16[514,256]{1,0:T(8,128)(2,1)S(1)}, bf16[514,256]{1,0:T(8,128)(2,1)S(1)}, u32[]{:S(2)}, u32[]{:S(2)}) %collective-permute-start.4) | collective-permute-done | bytes 263200 | tf_op jit(solution)/shard_map/ppermute | solution.py:25
  135.1 3.9 collective-permute-start.5
  139.0 15.6 %collective-permute-done.3 = bf16[514,512]{1,0:T(8,128)(2,1)} collective-permute-done((bf16[514,512]{1,0:T(8,128)(2,1)}, bf16[514,512]{1,0:T(8,128)(2,1)}, u32[]{:S(2)}, u32[]{:S(2)}) %collective-permute-start.3) | collective-permute-done | bytes 526368 | tf_op jit(solution)/shard_map/ppermute | solution.py:25
  154.6 5.4 %multiply_convert_fusion.1 = (bf16[514,1024]{1,0:T(8,128)(2,1)}, f32[514,1024]{1,0:T(8,128)}) fusion(f32[1024]{0:T(1024)} %param.29, bf16[1024,1024]{1,0:T(8,128)(2,1)} %all-gather.6.cloned.1.call-done, bf16[514,512]{1,0:T(8,128)(2,1)} %collective-permute-done.3, bf16[514,512]{1,0:T(8,128)(2,1)} %maximum_select_fusion.5, pred[]{:T(512)S(6)} %eq.4), kind=kOutput, calls=%fused_computation.15 | convolution fusion | flops 1085831168 | bytes 6311937 | tf_op jit(solution)/shard_map/dot_general | solution.py:188
  160.0 5.5 %collective-permute-done.5 = bf16[514,512]{1,0:T(8,128)(2,1)} collective-permute-done((bf16[514,512]{1,0:T(8,128)(2,1)}, bf16[514,512]{1,0:T(8,128)(2,1)}, u32[]{:S(2)}, u32[]{:S(2)}) %collective-permute-start.5) | collective-permute-done | bytes 526368 | tf_op jit(solution)/shard_map/ppermute | solution.py:25
  165.6 5.5 %convert_reduce_fusion = (f32[1024]{0:T(1024)}, bf16[514,1024]{1,0:T(8,128)(2,1)S(1)}) fusion(f32[514,1024]{1,0:T(8,128)} %get-tuple-element.71, f32[1024]{0:T(1024)S(1)} %copy-done.35, bf16[1024,1024]{1,0:T(8,128)(2,1)} %all-gather.8.cloned.1.call-done, bf16[514,512]{1,0:T(8,128)(2,1)} %collective-permute-done.5, ...), kind=kOutput, calls=%fused_computation.14 | convolution fusion | flops 1089514496 | bytes 6316033 | tf_op jit(solution)/shard_map/dot_general | solution.py:199
  174.4 4.2 convolution_convert_fusion.4
  178.8 22.2 %reduce-scatter.13.cloned.1.call-done = bf16[514,256]{1,0:T(8,128)(2,1)} async-done(((bf16[514,1024]{1,0:T(8,128)(2,1)}), bf16[514,256]{1,0:T(8,128)(2,1)}) %reduce-scatter.13.cloned.1.call-update) | async-done | bytes 263184 | tf_op jit(solution)/shard_map/reduce_scatter | solution.py:36
  203.0 10.0 %all-reduce.2 = (f32[514,1]{0,1:T(1,128)}, f32[514,1]{0,1:T(1,128)}) all-reduce(f32[514,1]{0,1:T(1,128)S(1)} %broadcast_in_dim.21, f32[514,1]{0,1:T(1,128)S(1)} %broadcast_in_dim.20), channel_id=1, replica_groups=mesh['img'=2,'row'=4,'col'=4] {'col'}, use_global_device_ids=true, to_apply=%region_16.17 | all-reduce | flops 1028 | bytes 8224 | tf_op jit(solution)/shard_map/psum | solution.py:42
  213.7 15.7 %reduce-scatter.11.cloned.1.call-done = bf16[514,256]{1,0:T(8,128)(2,1)} async-done(((bf16[514,1024]{1,0:T(8,128)(2,1)}), bf16[514,256]{1,0:T(8,128)(2,1)}) %reduce-scatter.11.cloned.1.call-update) | async-done | bytes 263184 | tf_op jit(solution)/shard_map/reduce_scatter | solution.py:36
  229.4 3.2 multiply_reduce_fusion.2
  233.5 7.7 %collective-permute-done.6 = bf16[514,256]{1,0:T(8,128)(2,1)S(1)} collective-permute-done((bf16[514,256]{1,0:T(8,128)(2,1)S(1)}, bf16[514,256]{1,0:T(8,128)(2,1)S(1)}, u32[]{:S(2)}, u32[]{:S(2)}) %collective-permute-start.6) | collective-permute-done | bytes 263200 | tf_op jit(solution)/shard_map/ppermute | solution.py:25
  242.8 23.6 %collective-permute-done.7 = bf16[514,512]{1,0:T(8,128)(2,1)S(1)} collective-permute-done((bf16[514,512]{1,0:T(8,128)(2,1)S(1)}, bf16[514,512]{1,0:T(8,128)(2,1)S(1)}, u32[]{:S(2)}, u32[]{:S(2)}) %collective-permute-start.7) | collective-permute-done | bytes 526368 | tf_op jit(solution)/shard_map/ppermute | solution.py:25
  268.8 5.1 %convolution_convert_fusion = bf16[1024,1024]{1,0:T(8,128)(2,1)} fusion(bf16[514,1024]{1,0:T(8,128)(2,1)} %get-tuple-element.70, bf16[514,512]{1,0:T(8,128)(2,1)} %collective-permute-done.5, bf16[514,512]{1,0:T(8,128)(2,1)} %maximum_select_fusion.6, pred[]{:T(512)S(6)} %eq.4), kind=kOutput, calls=%fused_computation.17 | convolution fusion | flops 1083721728 | bytes 4202497 | tf_op jit(solution)/shard_map/dot_general | solution.py:71
  273.9 5.1 %convolution_convert_fusion.1 = bf16[1024,1024]{1,0:T(8,128)(2,1)} fusion(bf16[514,1024]{1,0:T(8,128)(2,1)} %copy-done.36, bf16[514,512]{1,0:T(8,128)(2,1)} %collective-permute-done.3, bf16[514,512]{1,0:T(8,128)(2,1)} %maximum_select_fusion.5, pred[]{:T(512)S(6)} %eq.4), kind=kOutput, calls=%fused_computation.18 | convolution fusion | flops 1083721728 | bytes 4202497 | tf_op jit(solution)/shard_map/dot_general | solution.py:71
  286.3 3.0 fusion.11
  302.9 3.9 convolution_convert_fusion.2
  306.9 3.5 bitcast_convert_fusion
  310.5 12.3 %reduce-scatter.23.cloned.1.call-done = bf16[256,1024]{1,0:T(8,128)(2,1)} async-done(((bf16[1024,1024]{1,0:T(8,128)(2,1)}), bf16[256,1024]{1,0:T(8,128)(2,1)}) %reduce-scatter.23.cloned.1.call-update) | async-done | bytes 524304 | tf_op jit(solution)/shard_map/reduce_scatter | solution.py:228
  322.8 33.7 %reduce-scatter.21.cloned.1.call-done = bf16[256,1024]{1,0:T(8,128)(2,1)} async-done(((bf16[1024,1024]{1,0:T(8,128)(2,1)}), bf16[256,1024]{1,0:T(8,128)(2,1)}) %reduce-scatter.21.cloned.1.call-update) | async-done | bytes 524304 | tf_op jit(solution)/shard_map/reduce_scatter | solution.py:225
  356.5 30.5 %reduce-scatter.17.cloned.1.call-done = bf16[256,3,256]{2,0,1:T(8,128)(2,1)} async-done(((bf16[1024,3,256]{2,0,1:T(8,128)(2,1)}), bf16[256,3,256]{2,0,1:T(8,128)(2,1)}) %reduce-scatter.17.cloned.1.call-update) | async-done | bytes 393232 | tf_op jit(solution)/shard_map/reduce_scatter | solution.py:219
  387.4 29.7 %reduce-scatter.15.cloned.1.call-done = bf16[514,256]{1,0:T(8,128)(2,1)} async-done(((bf16[514,1024]{1,0:T(8,128)(2,1)}), bf16[514,256]{1,0:T(8,128)(2,1)}) %reduce-scatter.15.cloned.1.call-update) | async-done | bytes 263184 | tf_op jit(solution)/shard_map/reduce_scatter | solution.py:36
  418.6 24.8 %all-reduce = (f32[2,256]{1,0:T(2,128)}, f32[256]{0:T(256)}, f32[256]{0:T(256)}, f32[1024]{0:T(1024)}, f32[256]{0:T(256)}, /*index=5*/f32[256]{0:T(256)}, f32[25...) all-reduce(f32[2,256]{1,0:T(2,128)S(1)} %pad_maximum_fusion, ...), channel_id=1, replica_groups=mesh['img'=2,'row'=4,'col'=4] {'img','row'}, use_global_device_ids=true, to_apply=%region_27.28 | all-reduce | flops 3584 | bytes 28672 | tf_op jit(solution)/shard_map/psum | solution.py:239
  443.3 9.2 %all-reduce.1 = (f32[514,1]{0,1:T(1,128)S(1)}, f32[514,1]{0,1:T(1,128)S(1)}) all-reduce(f32[514,1]{0,1:T(1,128)S(1)} %broadcast_in_dim.23, f32[514,1]{0,1:T(1,128)S(1)} %broadcast_in_dim.22), channel_id=1, replica_groups=mesh['img'=2,'row'=4,'col'=4] {'col'}, use_global_device_ids=true, to_apply=%region_22.23 | all-reduce | flops 1028 | bytes 8224 | tf_op jit(solution)/shard_map/psum | solution.py:42
  454.6 15.0 %all-reduce.8.cloned.1.call-done = (bf16[256,3,256]{2,0,1:T(8,128)(2,1)}, bf16[256,256]{1,0:T(8,128)(2,1)}, bf16[256,1024]{1,0:T(8,128)(2,1)}, bf16[256,1024]{1,0:T(8,128)(2,1)}) async-done(((bf16[256,3,256]{2,0,1:T(8,128)(2,1)}, bf16[256,256]{1,0:T(8,128)(2,1)}, bf16[256,1024]{1,0:T(8,128)(2,1)}, bf16[256,1024]{1,0:T(8,128)(2,1)}), (bf16[256,3,256]{2,0,1:T(8,128)(2,1)}, bf16[256,256]{1,0:T(8,128)(2,1)}, ...) | async-done | bytes 1572880 | tf_op jit(solution)/shard_map/psum | solution.py:233
  (179 shorter events, 76.5 us)
Async XLA Ops:
  7.2 46.7 %all-gather.4.cloned.1.call-start = ((), (), s32[]{:S(2)}) async-start(), calls=%async_computation.8 | async-start | bytes 1966080 | tf_op jit(solution)/shard_map/all_gather | solution.py:171
  7.9 90.6 %reduce-scatter.9.cloned.1.call-start = ((), (), s32[]{:S(2)}) async-start(), calls=%async_computation.9 | async-start | bytes 1331200 | tf_op jit(solution)/shard_map/reduce_scatter | solution.py:36
  24.3 6.5 %collective-permute-start = (bf16[514,256]{1,0:T(8,128)(2,1)S(1)}, bf16[514,256]{1,0:T(8,128)(2,1)S(1)}, u32[]{:S(2)}, u32[]{:S(2)}) collective-permute-start(bf16[514,256]{1,0:T(8,128)(2,1)S(1)} %fusion.38), channel_id=1, source_target_pairs={{0,1},{1,0},{2,3},{3,2},{4,5},{5,4},{6,7},{7,6},{8,9},{9,8},{10,11... | collective-permute-start | bytes 789512 | tf_op jit(solution)/shard_map/ppermute | solution.py:25
  30.9 23.0 %collective-permute-start.1 = (bf16[514,512]{1,0:T(8,128)(2,1)S(1)}, bf16[514,512]{1,0:T(8,128)(2,1)S(1)}, u32[]{:S(2)}, u32[]{:S(2)}) collective-permute-start(bf16[514,512]{1,0:T(8,128)(2,1)S(1)} %maximum_select_fusion.4), channel_id=1, source_target_pairs={{0,2},{1,3},{2,0},{3,1},{4,6},{5,7},{6,4},{7,5},{8,10},{9,11},{10,... | collective-permute-start | bytes 1579016 | tf_op jit(solution)/shard_map/ppermute | solution.py:25
  69.7 41.1 %copy-start.22 = (f32[256]{0:T(256)S(1)}, f32[256]{0:T(256)}, u32[]{:S(2)}) copy-start(f32[256]{0:T(256)} %param.26) | copy-start | bytes 3076
  72.4 66.6 %all-gather.6.cloned.1.call-start = ((), (), s32[]{:S(2)}) async-start(), calls=%async_computation.10 | async-start | bytes 2621440 | tf_op jit(solution)/shard_map/all_gather | solution.py:173
  73.2 92.4 %all-gather.8.cloned.1.call-start = ((), (), s32[]{:S(2)}) async-start(), calls=%async_computation.11 | async-start | bytes 2621440 | tf_op jit(solution)/shard_map/all_gather | solution.py:174
  73.8 127.2 %reduce-scatter.13.cloned.1.call-start = ((), (), s32[]{:S(2)}) async-start(), calls=%async_computation.13 | async-start | bytes 1331200 | tf_op jit(solution)/shard_map/reduce_scatter | solution.py:36
  112.0 6.5 %collective-permute-start.2 = (bf16[514,256]{1,0:T(8,128)(2,1)S(1)}, bf16[514,256]{1,0:T(8,128)(2,1)S(1)}, u32[]{:S(2)}, u32[]{:S(2)}) collective-permute-start(bf16[514,256]{1,0:T(8,128)(2,1)S(1)} %add_convert_fusion), channel_id=1, source_target_pairs={{0,1},{1,0},{2,3},{3,2},{4,5},{5,4},{6,7},{7,6},{8,9},{9,8},{10,11... | collective-permute-start | bytes 789512 | tf_op jit(solution)/shard_map/ppermute | solution.py:25
  119.4 35.2 %collective-permute-start.3 = (bf16[514,512]{1,0:T(8,128)(2,1)}, bf16[514,512]{1,0:T(8,128)(2,1)}, u32[]{:S(2)}, u32[]{:S(2)}) collective-permute-start(bf16[514,512]{1,0:T(8,128)(2,1)} %maximum_select_fusion.5), channel_id=1, source_target_pairs={{0,2},{1,3},{2,0},{3,1},{4,6},{5,7},{6,4},{7,5},{8,10},{9,11},{10,... | collective-permute-start | bytes 1579016 | tf_op jit(solution)/shard_map/ppermute | solution.py:25
  120.1 14.0 %collective-permute-start.4 = (bf16[514,256]{1,0:T(8,128)(2,1)S(1)}, bf16[514,256]{1,0:T(8,128)(2,1)S(1)}, u32[]{:S(2)}, u32[]{:S(2)}) collective-permute-start(bf16[514,256]{1,0:T(8,128)(2,1)S(1)} %multiply_convert_fusion.3), channel_id=1, source_target_pairs={{0,1},{1,0},{2,3},{3,2},{4,5},{5,4},{6,7},{7,6},{8,9},{9,8},{10,11... | collective-permute-start | bytes 789512 | tf_op jit(solution)/shard_map/ppermute | solution.py:25
  135.1 30.5 %copy-start.35 = (f32[1024]{0:T(1024)S(1)}, f32[1024]{0:T(1024)}, u32[]{:S(2)}) copy-start(f32[1024]{0:T(1024)} %param.29) | copy-start | bytes 12292
  135.1 30.5 %collective-permute-start.5 = (bf16[514,512]{1,0:T(8,128)(2,1)}, bf16[514,512]{1,0:T(8,128)(2,1)}, u32[]{:S(2)}, u32[]{:S(2)}) collective-permute-start(bf16[514,512]{1,0:T(8,128)(2,1)} %maximum_select_fusion.6), channel_id=1, source_target_pairs={{0,2},{1,3},{2,0},{3,1},{4,6},{5,7},{6,4},{7,5},{8,10},{9,11},{10,... | collective-permute-start | bytes 1579016 | tf_op jit(solution)/shard_map/ppermute | solution.py:25
  174.4 55.0 %reduce-scatter.11.cloned.1.call-start = ((), (), s32[]{:S(2)}) async-start(), calls=%async_computation.12 | async-start | bytes 1331200 | tf_op jit(solution)/shard_map/reduce_scatter | solution.py:36
  178.7 131.8 %reduce-scatter.19.cloned.1.call-start = ((), (), s32[]{:S(2)}) async-start(), calls=%async_computation.16 | async-start | bytes 655360 | tf_op jit(solution)/shard_map/reduce_scatter | solution.py:222
  229.4 37.7 %copy-start.12 = (bf16[514,256]{0,1:T(8,128)(2,1)S(1)}, bf16[514,256]{0,1:T(8,128)(2,1)}, u32[]{:S(2)}) copy-start(bf16[514,256]{0,1:T(8,128)(2,1)} %convert_element_type.114) | copy-start | bytes 789508
  233.4 7.8 %collective-permute-start.6 = (bf16[514,256]{1,0:T(8,128)(2,1)S(1)}, bf16[514,256]{1,0:T(8,128)(2,1)S(1)}, u32[]{:S(2)}, u32[]{:S(2)}) collective-permute-start(bf16[514,256]{1,0:T(8,128)(2,1)S(1)} %multiply_convert_fusion.2), channel_id=1, source_target_pairs={{0,1},{1,0},{2,3},{3,2},{4,5},{5,4},{6,7},{7,6},{8,9},{9,8},{10,11... | collective-permute-start | bytes 789512 | tf_op jit(solution)/shard_map/ppermute | solution.py:25
  241.4 25.0 %collective-permute-start.7 = (bf16[514,512]{1,0:T(8,128)(2,1)S(1)}, bf16[514,512]{1,0:T(8,128)(2,1)S(1)}, u32[]{:S(2)}, u32[]{:S(2)}) collective-permute-start(bf16[514,512]{1,0:T(8,128)(2,1)S(1)} %maximum_select_fusion.7), channel_id=1, source_target_pairs={{0,2},{1,3},{2,0},{3,1},{4,6},{5,7},{6,4},{7,5},{8,10},{9,11},{10,... | collective-permute-start | bytes 1579016 | tf_op jit(solution)/shard_map/ppermute | solution.py:25
  268.7 54.1 %reduce-scatter.23.cloned.1.call-start = ((), (), s32[]{:S(2)}) async-start(), calls=%async_computation.18 | async-start | bytes 2621440 | tf_op jit(solution)/shard_map/reduce_scatter | solution.py:228
  273.9 82.6 %reduce-scatter.21.cloned.1.call-start = ((), (), s32[]{:S(2)}) async-start(), calls=%async_computation.17 | async-start | bytes 2621440 | tf_op jit(solution)/shard_map/reduce_scatter | solution.py:225
  279.1 108.0 %reduce-scatter.17.cloned.1.call-start = ((), (), s32[]{:S(2)}) async-start(), calls=%async_computation.15 | async-start | bytes 1966080 | tf_op jit(solution)/shard_map/reduce_scatter | solution.py:219
  306.9 110.2 %reduce-scatter.15.cloned.1.call-start = ((), (), s32[]{:S(2)}) async-start(), calls=%async_computation.14 | async-start | bytes 1331200 | tf_op jit(solution)/shard_map/reduce_scatter | solution.py:36
  310.4 159.3 %all-reduce.8.cloned.1.call-start = ((), (), s32[]{:S(2)}) async-start(), calls=%async_computation.19 | async-start | bytes 3145728 | tf_op jit(solution)/shard_map/psum | solution.py:233
  387.0 30.0 %copy-start.23 = (f32[256]{0:T(256)S(1)}, f32[256]{0:T(256)}, u32[]{:S(2)}) copy-start(f32[256]{0:T(256)} %param.19) | copy-start | bytes 3076
  387.0 31.4 %copy-start.24 = (f32[256]{0:T(256)S(1)}, f32[256]{0:T(256)}, u32[]{:S(2)}) copy-start(f32[256]{0:T(256)} %get-tuple-element.26) | copy-start | bytes 3076
  387.1 31.4 %copy-start.25 = (f32[256]{0:T(256)S(1)}, f32[256]{0:T(256)}, u32[]{:S(2)}) copy-start(f32[256]{0:T(256)} %get-tuple-element.27) | copy-start | bytes 3076
  387.1 31.4 %copy-start.26 = (f32[256]{0:T(256)S(1)}, f32[256]{0:T(256)}, u32[]{:S(2)}) copy-start(f32[256]{0:T(256)} %get-tuple-element.64) | copy-start | bytes 3076
  387.1 31.4 %copy-start.27 = (f32[256]{0:T(256)S(1)}, f32[256]{0:T(256)}, u32[]{:S(2)}) copy-start(f32[256]{0:T(256)} %get-tuple-element.65) | copy-start | bytes 3076
  387.1 31.4 %copy-start.28 = (f32[256]{0:T(256)S(1)}, f32[256]{0:T(256)}, u32[]{:S(2)}) copy-start(f32[256]{0:T(256)} %get-tuple-element.18) | copy-start | bytes 3076
  387.1 31.4 %copy-start.29 = (f32[256]{0:T(256)S(1)}, f32[256]{0:T(256)}, u32[]{:S(2)}) copy-start(f32[256]{0:T(256)} %get-tuple-element.30) | copy-start | bytes 3076
  387.1 31.4 %copy-start.30 = (f32[1024]{0:T(1024)S(1)}, f32[1024]{0:T(1024)}, u32[]{:S(2)}) copy-start(f32[1024]{0:T(1024)} %get-tuple-element.74) | copy-start | bytes 12292
  387.1 65.4 %copy-start.7 = (f32[514,256]{1,0:T(8,128)S(1)}, f32[514,256]{1,0:T(8,128)}, u32[]{:S(2)}) copy-start(f32[514,256]{1,0:T(8,128)} %copy-done.6) | copy-start | bytes 1579012
  (25 other events, 243.5 us)
Sparse Core Ops, SparseCore 0:
  9.6 22.3 all-gather.3
  72.6 25.9 reduce-scatter.8
  100.1 21.0 all-gather.5
  122.6 22.5 all-gather.7
  174.5 26.3 reduce-scatter.12
  203.1 26.3 reduce-scatter.10
  268.8 20.2 reduce-scatter.18
  291.6 31.1 reduce-scatter.22
  325.3 31.1 reduce-scatter.20
  358.9 28.0 reduce-scatter.16
  389.3 27.6 reduce-scatter.14
  419.4 50.2 all-reduce.7
